TPU v7x, 512 devices: a whole 4x8x8 slice. The times are simulated.
512 devices in a mesh: row: 8 (over z_lo, core), bulk: 64 (over z_hi, x, y).
Axes of the slice: x: 4, y: 8, z: 8 (z_hi: 2, z_lo: 4; z = z_hi * 4 + z_lo), core: 2. Of those that a mesh axis runs over, the one named last changes fastest.
Arguments:
- residual_in: float32 [2048, 65536], P('row', 'bulk'), may hold values from -6 to 6
- amplitudes: float32 [2048, 2048], P('row', 'bulk'), may hold values from -6 to 6
- integral_tiles: float32 [4096, 128, 128], P('bulk', 'row'), may hold values from -0.1875 to 0.1875
- tile_reader: int32 [4096, 1], P('bulk'), may hold values from 0 to 63; in each aligned block of 64 rows (0 to 63, 64 to 127, ...) at most 2 rows name the same one
- tile_k: int32 [4096], P('bulk'), may hold values from 0 to 15
- tile_column: int32 [4096], P('bulk'), may hold values from 0 to 7
Outputs:
- residual_out: float32 [2048, 65536], P('row', 'bulk')
Inputs may be any that keep to these rules, and one draw needn't show every extreme that they name: `tile_reader`: among the 64 tiles stored on one index of bulk (aligned blocks of 64 entries), at most 2 name the same reader; some block has exactly 2 for some reader.
All inputs are finite; a program needn't handle non-finite values.
Results may differ from a plain program's by a relative error of at most 0.0003.
Values sent between devices are 32-bit elements; how exact they have to be, the bound alone decides.
A program may use at most 64 MiB of HBM per device.

v0:
```python
import jax
import jax.numpy as jnp
from jax import lax
from jax.sharding import PartitionSpec as P

KT = 16
CT = 8
SLOT = 2


def bucket_slots(tile_reader, tile_k, tile_column, targets, slots):
    readers = tile_reader[:, 0]
    matches = (readers[:, None] == jnp.arange(targets, dtype=jnp.int32)[None, :]).astype(jnp.int32)
    ordinal = jnp.cumsum(matches, axis=0) - matches
    position = jnp.sum(ordinal * matches, axis=1)
    select = matches.T[:, None, :] * (
        position[None, None, :] == jnp.arange(slots, dtype=jnp.int32)[None, :, None]
    ).astype(jnp.int32)
    filled = jnp.sum(select, axis=2)
    slot_tile = jnp.sum(select * tile_k[None, None, :], axis=2) + filled - 1
    slot_column = jnp.sum(select * tile_column[None, None, :], axis=2) + filled - 1
    return (select.astype(jnp.float32), slot_tile, slot_column)


def pair_table(slot_tile, slot_column, tiles_count, column_count):
    tile_hot = (slot_tile[:, None] == jnp.arange(tiles_count, dtype=jnp.int32)[None, :]).astype(
        jnp.float32
    )
    column_hot = (
        slot_column[:, None] == jnp.arange(column_count, dtype=jnp.int32)[None, :]
    ).astype(jnp.float32)
    return (tile_hot[:, :, None] * column_hot[:, None, :]).reshape(
        slot_tile.shape[0], tiles_count * column_count
    )


def place_rows(table, portion, tiles_count, column_count):
    width = portion.shape[2]
    height = portion.shape[1]
    placed = jnp.dot(
        table.T, portion.reshape(portion.shape[0], height * width), precision=lax.Precision.HIGHEST
    )
    placed = placed.reshape(tiles_count, column_count, height, width).transpose(0, 2, 1, 3)
    return placed


def local(residual_in, amplitudes, integral_tiles, tile_reader, tile_k, tile_column):
    targets = lax.axis_size("bulk")
    select, slot_tile, slot_column = bucket_slots(tile_reader, tile_k, tile_column, targets, SLOT)
    width = integral_tiles.shape[2]
    whole_tiles = lax.all_gather(integral_tiles, "row", axis=1, tiled=True)
    outgoing = jnp.einsum("dsj,jpq->dspq", select, whole_tiles, precision=lax.Precision.HIGHEST)
    arrived, arrived_tile, arrived_column = (
        lax.all_to_all(outgoing, "bulk", split_axis=0, concat_axis=0, tiled=True),
        lax.all_to_all(slot_tile, "bulk", split_axis=0, concat_axis=0, tiled=True),
        lax.all_to_all(slot_column, "bulk", split_axis=0, concat_axis=0, tiled=True),
    )
    arrived = arrived.reshape(targets * SLOT, width, width)
    table = pair_table(arrived_tile.reshape(-1), arrived_column.reshape(-1), KT, CT)
    assembled = place_rows(table, arrived, KT, CT)
    dense_block = assembled.reshape(KT * width, CT * width)
    return residual_in + jnp.dot(
        lax.all_gather(amplitudes, "bulk", axis=1, tiled=True),
        dense_block,
        precision=lax.Precision.HIGHEST,
    )


def solution(mesh):
    placed = (
        P("row", "bulk"),
        P("row", "bulk"),
        P("bulk", "row", None),
        P("bulk", None),
        P("bulk"),
        P("bulk"),
    )
    return jax.shard_map(
        local, mesh=mesh, in_specs=placed, out_specs=P("row", "bulk"), check_vma=False
    )
```

profile of v0, /device:TPU:2, one launch (start us, length us, event | category | flops | bytes accessed | tf_op | source)
XLA Modules:
  0.0 432.5 jit_solution(5636964937242267138)
XLA Ops:
  7.4 0.0 all-gather.3.cloned.1.call-start
  7.4 2.0 copy.21
  9.4 0.0 all-gather.3.cloned.1.call-update
  9.4 0.8 fusion.23
  10.2 0.1 reduce_window_sum.11
  10.3 0.8 select_reduce_fusion
  11.2 0.9 fusion.11
  12.0 0.7 copy.19
  12.7 19.1 %all-to-all-start = ((s32[64,1,2]{2,1,0:T(1,128)}), s32[64,1,2]{2,1,0:T(1,128)S(1)}, u32[]{:S(2)}, u32[]{:S(2)}) async-start(s32[64,1,2]{2,1,0:T(1,128)} %copy.19), calls=%async_computation | async-start | bytes 65536 | tf_op jit(solution)/shard_map/all_to_all | solution.py:55
  31.8 0.7 copy.20
  32.5 12.7 %all-to-all-done = s32[64,1,2]{2,1,0:T(1,128)S(1)} async-done(((s32[64,1,2]{2,1,0:T(1,128)}), s32[64,1,2]{2,1,0:T(1,128)S(1)}, u32[]{:S(2)}, u32[]{:S(2)}) %all-to-all-start) | async-done | bytes 544 | tf_op jit(solution)/shard_map/all_to_all | solution.py:55
  45.3 5.4 %all-to-all-start.1 = ((s32[64,1,2]{2,1,0:T(1,128)}), s32[64,1,2]{2,1,0:T(1,128)S(1)}, u32[]{:S(2)}, u32[]{:S(2)}) async-start(s32[64,1,2]{2,1,0:T(1,128)} %copy.20), calls=%async_computation.1 | async-start | bytes 65536 | tf_op jit(solution)/shard_map/all_to_all | solution.py:56
  50.7 23.5 %all-gather.3.cloned.1.call-done = f32[64,128,128]{2,0,1:T(8,128)} async-done(((f32[64,16,128]{2,0,1:T(8,128)}), f32[64,128,128]{2,0,1:T(8,128)}) %all-gather.3.cloned.1.call-update) | async-done | bytes 4194320 | tf_op jit(solution)/shard_map/all_gather | solution.py:51
  74.2 8.7 %fusion.3 = f32[64,2,128,128]{3,0,2,1:T(8,128)S(1)} fusion(f32[64,128,128]{2,0,1:T(8,128)} %all-gather.3.cloned.1.call-done, s32[2,64]{1,0:T(2,128)S(1)} %compare_convert_fusion, s32[64,64]{1,0:T(8,128)S(1)} %get-tuple-element.10), kind=kOutput, calls=%fused_computation.4 | convolution fusion | flops 1610629120 | bytes 12599808 | tf_op jit(solution)/shard_map/dsj,jpq->dspq/dot_general | solution.py:52
  82.9 8.1 %copy.22 = f32[64,2,128,128]{3,2,1,0:T(8,128)} copy(f32[64,2,128,128]{3,0,2,1:T(8,128)S(1)} %fusion.3) | data formatting | bytes 16777216 | tf_op jit(solution)/shard_map/dsj,jpq->dspq/dot_general | solution.py:52
  91.0 0.0 copy-start
  91.0 0.0 all-to-all-done.1
  91.0 13.4 %all-to-all-start.2 = ((f32[64,2,128,128]{3,2,1,0:T(8,128)}), f32[64,2,128,128]{3,2,1,0:T(8,128)}, u32[]{:S(2)}, u32[]{:S(2)}) async-start(f32[64,2,128,128]{3,2,1,0:T(8,128)} %copy.22), calls=%async_computation.2 | async-start | bytes 16777216 | tf_op jit(solution)/shard_map/all_to_all | solution.py:54
  104.4 0.0 all-gather.5.cloned.1.call-start
  104.5 0.5 all-gather.5.cloned.1.call-update
  105.0 0.0 copy-done
  105.0 0.3 copy.24
  105.3 0.5 broadcast.89
  105.9 0.7 reduce.7
  106.6 0.1 eq.92
  106.7 0.7 reduce.6
  107.5 0.1 eq.96
  107.6 236.8 %all-to-all-done.2 = f32[64,2,128,128]{3,2,1,0:T(8,128)} async-done(((f32[64,2,128,128]{3,2,1,0:T(8,128)}), f32[64,2,128,128]{3,2,1,0:T(8,128)}, u32[]{:S(2)}, u32[]{:S(2)}) %all-to-all-start.2) | async-done | bytes 8388640 | tf_op jit(solution)/shard_map/all_to_all | solution.py:54
  344.4 13.2 %copy.39 = f32[16,8,128,128]{3,1,2,0:T(8,128)} copy(f32[16,8,128,128]{3,2,1,0:T(8,128)} %bitcast.23) | data formatting | bytes 16777216
  357.6 9.0 %copy.23 = f32[16384,128]{1,0:T(8,128)} copy(f32[16384,128]{0,1:T(8,128)} %bitcast.53) | data formatting | bytes 16777216 | tf_op jit(solution)/shard_map/dot_general | solution.py:40
  366.6 12.1 %fusion.15 = f32[16,8,128,128]{3,1,2,0:T(8,128)} fusion(f32[128,128,128,1]{2,1,0,3:T(8,128)} %bitcast.52, f32[128,8]{0,1:T(8,128)S(1)} %fusion.25, f32[128,16]{0,1:T(8,128)S(1)} %fusion.24), kind=kOutput, calls=%fused_computation.15 | convolution fusion | flops 3221241856 | bytes 16789504 | tf_op jit(solution)/shard_map/dot_general | solution.py:40
  378.6 28.0 %all-gather.5.cloned.1.call-done = f32[256,2048]{0,1:T(8,128)} async-done(((f32[256,32]{0,1:T(8,128)}), f32[256,2048]{0,1:T(8,128)}) %all-gather.5.cloned.1.call-update) | async-done | bytes 2097168 | tf_op jit(solution)/shard_map/all_gather | solution.py:63
  406.7 17.1 %fusion.8 = f32[256,1024]{0,1:T(8,128)S(1)} fusion(f32[256,1024]{0,1:T(8,128)S(1)} %copy.24, f32[256,2048]{0,1:T(8,128)} %all-gather.5.cloned.1.call-done, f32[256,8,8,128]{3,2,1,0:T(8,128)} %bitcast.51), kind=kOutput, calls=%fused_computation.7 | convolution fusion | flops 6442713088 | bytes 12582912 | tf_op jit(solution)/shard_map/dot_general | solution.py:62
  423.7 1.3 copy.25
  (4 shorter events, 0.0 us)
Async XLA Ops:
  7.4 66.8 %all-gather.3.cloned.1.call-start = ((), (), s32[]{:S(2)}) async-start(), calls=%async_computation.3 | async-start | bytes 4718592 | tf_op jit(solution)/shard_map/all_gather | solution.py:51
  12.7 32.5 %all-to-all-start = ((s32[64,1,2]{2,1,0:T(1,128)}), s32[64,1,2]{2,1,0:T(1,128)S(1)}, u32[]{:S(2)}, u32[]{:S(2)}) async-start(s32[64,1,2]{2,1,0:T(1,128)} %copy.19), calls=%async_computation | async-start | bytes 65536 | tf_op jit(solution)/shard_map/all_to_all | solution.py:55
  45.3 45.7 %all-to-all-start.1 = ((s32[64,1,2]{2,1,0:T(1,128)}), s32[64,1,2]{2,1,0:T(1,128)S(1)}, u32[]{:S(2)}, u32[]{:S(2)}) async-start(s32[64,1,2]{2,1,0:T(1,128)} %copy.20), calls=%async_computation.1 | async-start | bytes 65536 | tf_op jit(solution)/shard_map/all_to_all | solution.py:56
  91.0 14.0 %copy-start = (f32[256,1024]{1,0:T(8,128)S(1)}, f32[256,1024]{1,0:T(8,128)}, u32[]{:S(2)}) copy-start(f32[256,1024]{1,0:T(8,128)} %param.6) | copy-start | bytes 3145732
  91.0 253.4 %all-to-all-start.2 = ((f32[64,2,128,128]{3,2,1,0:T(8,128)}), f32[64,2,128,128]{3,2,1,0:T(8,128)}, u32[]{:S(2)}, u32[]{:S(2)}) async-start(f32[64,2,128,128]{3,2,1,0:T(8,128)} %copy.22), calls=%async_computation.2 | async-start | bytes 16777216 | tf_op jit(solution)/shard_map/all_to_all | solution.py:54
  104.4 302.2 %all-gather.5.cloned.1.call-start = ((), (), s32[]{:S(2)}) async-start(), calls=%async_computation.4 | async-start | bytes 2129920 | tf_op jit(solution)/shard_map/all_gather | solution.py:63
Sparse Core Ops, SparseCore 0:
  10.3 63.8 all-gather.2
Sparse Core Ops, SparseCore 1:
  109.4 297.2 all-gather.4
where the time goes:
time: 433 us; the launch traced here: 432 us
  waiting for transfers between devices  302 us (70%)
  starting transfers between devices  38 us (9%)
  matrix products  37.9 us (9%)
  local copies, waits for them, and re-layouts  36.1 us (8%)
  between operations  15 us (3%)
    all_to_all x1, waiting for transfers between devices, local(): lax.all_to_all(outgoing, 'bulk', split_axis=0, concat_axis=0, tiled=True)  237 us
    all_gather x1, waiting for transfers between devices, local(): lax.all_gather(amplitudes, 'bulk', axis=1, tiled=True)  28 us
    all_gather x1, waiting for transfers between devices, local(): whole_tiles = lax.all_gather(integral_tiles, 'row', axis=1, tiled=True)  23.5 us
    all_to_all x1, starting transfers between devices, local(): lax.all_to_all(slot_tile, 'bulk', split_axis=0, concat_axis=0, tiled=True)  19.1 us
    dot_general x1, matrix products, local(): jnp.dot(lax.all_gather(amplitudes, 'bulk', axis=1, tiled=True), dense_blo...  17.1 us
    unnamed x5, local copies, waits for them, and re-layouts  15.5 us
    all_to_all x1, starting transfers between devices, local(): lax.all_to_all(outgoing, 'bulk', split_axis=0, concat_axis=0, tiled=True)  13.4 us
    all_to_all x1, waiting for transfers between devices, local(): lax.all_to_all(slot_tile, 'bulk', split_axis=0, concat_axis=0, tiled=True)  12.7 us
  transfers between devices with their start and end apart: 5, of which 4 were waited for; matrix products, arithmetic and copies ran while one was open for 13% of the time, Pallas kernels for 0%

commit v1 on v0

--- a/solution.py
+++ b/solution.py
@@ -60,7 +60,15 @@
     assembled = place_rows(table, arrived, KT, CT)
     dense_block = assembled.reshape(KT * width, CT * width)
     return residual_in + jnp.dot(
-        lax.all_gather(amplitudes, "bulk", axis=1, tiled=True),
+        jnp.concatenate(
+            lax.all_to_all(
+                jnp.stack([amplitudes for _ in range(lax.axis_size("bulk"))], axis=0),
+                axis_name="bulk",
+                split_axis=0,
+                concat_axis=0,
+            ),
+            1,
+        ),
         dense_block,
         precision=lax.Precision.HIGHEST,
     )

time: 433 us -> 396 us (0.915)
  the two profiles are of different devices: /device:TPU:2 before, /device:TPU:142 now
where the time goes in v1:
time: 396 us
  blocking collectives  205 us (52%)
  waiting for transfers between devices  47.6 us (12%)
  starting transfers between devices  46.5 us (12%)
  local copies, waits for them, and re-layouts  40.1 us (10%)
  matrix products  38.6 us (10%)
  between operations  13.5 us (3%)
  other arithmetic  4.07 us (1%)
    all_to_all x1, blocking collectives, local(): lax.all_to_all(outgoing, 'bulk', split_axis=0, concat_axis=0, tiled=True)  205 us
    all_to_all x1, starting transfers between devices, local(): lax.all_to_all(jnp.stack([amplitudes for _ in range(lax.axis_size('bulk')...  22.4 us
    all_gather x1, waiting for transfers between devices, local(): whole_tiles = lax.all_gather(integral_tiles, 'row', axis=1, tiled=True)  19.8 us
    dot_general x1, matrix products, local(): jnp.dot(jnp.concatenate(lax.all_to_all(jnp.stack([amplitudes for _ in ran...  17.8 us
    all_to_all x1, starting transfers between devices, local(): lax.all_to_all(slot_tile, 'bulk', split_axis=0, concat_axis=0, tiled=True)  17.2 us
    unnamed x5, local copies, waits for them, and re-layouts  16.7 us
    all_to_all x1, waiting for transfers between devices, local(): lax.all_to_all(jnp.stack([amplitudes for _ in range(lax.axis_size('bulk')...  16.5 us
    dot_general x1, matrix products, place_rows(): jnp.dot(table.T, portion.reshape(portion.shape[0], height * width), preci...  12.1 us
  transfers between devices with their start and end apart: 4, of which 3 were waited for; matrix products, arithmetic and copies ran while one was open for 15% of the time, Pallas kernels for 0%

profile of v1, /device:TPU:142, one launch (start us, length us, event | category | flops | bytes accessed | tf_op | source)
XLA Modules:
  0.0 395.6 jit_solution(8894293371314375349)
XLA Ops:
  6.5 0.0 all-gather.2.cloned.1.call-start
  6.5 2.0 copy.22
  8.5 0.0 all-gather.2.cloned.1.call-update
  8.6 0.8 fusion.23
  9.4 0.1 reduce_window_sum.11
  9.5 0.8 select_reduce_fusion
  10.3 0.9 fusion.11
  11.2 0.7 copy.20
  11.9 17.2 %all-to-all-start = ((s32[64,1,2]{2,1,0:T(1,128)}), s32[64,1,2]{2,1,0:T(1,128)S(1)}, u32[]{:S(2)}, u32[]{:S(2)}) async-start(s32[64,1,2]{2,1,0:T(1,128)} %copy.20), calls=%async_computation | async-start | bytes 65536 | tf_op jit(solution)/shard_map/all_to_all | solution.py:55
  29.1 0.7 copy.21
  29.8 11.3 %all-to-all-done = s32[64,1,2]{2,1,0:T(1,128)S(1)} async-done(((s32[64,1,2]{2,1,0:T(1,128)}), s32[64,1,2]{2,1,0:T(1,128)S(1)}, u32[]{:S(2)}, u32[]{:S(2)}) %all-to-all-start) | async-done | bytes 544 | tf_op jit(solution)/shard_map/all_to_all | solution.py:55
  41.1 6.9 %all-to-all-start.1 = ((s32[64,1,2]{2,1,0:T(1,128)}), s32[64,1,2]{2,1,0:T(1,128)S(1)}, u32[]{:S(2)}, u32[]{:S(2)}) async-start(s32[64,1,2]{2,1,0:T(1,128)} %copy.21), calls=%async_computation.1 | async-start | bytes 65536 | tf_op jit(solution)/shard_map/all_to_all | solution.py:56
  48.0 19.8 %all-gather.2.cloned.1.call-done = f32[64,128,128]{2,0,1:T(8,128)} async-done(((f32[64,16,128]{2,0,1:T(8,128)}), f32[64,128,128]{2,0,1:T(8,128)}) %all-gather.2.cloned.1.call-update) | async-done | bytes 4194320 | tf_op jit(solution)/shard_map/all_gather | solution.py:51
  67.8 8.7 %fusion.3 = f32[64,2,128,128]{3,0,2,1:T(8,128)S(1)} fusion(f32[64,128,128]{2,0,1:T(8,128)} %all-gather.2.cloned.1.call-done, s32[2,64]{1,0:T(2,128)S(1)} %compare_convert_fusion, s32[64,64]{1,0:T(8,128)S(1)} %get-tuple-element.10), kind=kOutput, calls=%fused_computation.4 | convolution fusion | flops 1610629120 | bytes 12599808 | tf_op jit(solution)/shard_map/dsj,jpq->dspq/dot_general | solution.py:52
  76.6 8.1 %copy.23 = f32[64,2,128,128]{3,2,1,0:T(8,128)} copy(f32[64,2,128,128]{3,0,2,1:T(8,128)S(1)} %fusion.3) | data formatting | bytes 16777216 | tf_op jit(solution)/shard_map/dsj,jpq->dspq/dot_general | solution.py:52
  84.7 0.0 copy-start
  84.7 0.0 all-to-all-done.1
  84.7 205.2 %all_to_all.22 = f32[64,2,128,128]{3,2,1,0:T(8,128)} all-to-all(f32[64,2,128,128]{3,2,1,0:T(8,128)} %copy.23), channel_id=1, replica_groups=mesh['row'=8,'bulk'=64] {'bulk'}, dimensions={0} | all-to-all | bytes 16777216 | tf_op jit(solution)/shard_map/all_to_all | solution.py:54
  289.8 0.0 copy-done
  289.8 1.6 stack.2
  291.5 22.4 %all-to-all-start.3 = ((f32[64,256,32]{1,2,0:T(8,128)}), f32[64,256,32]{1,2,0:T(8,128)S(1)}, u32[]{:S(2)}, u32[]{:S(2)}) async-start(f32[64,256,32]{1,2,0:T(8,128)} %stack.2), calls=%async_computation.3 | async-start | bytes 4194304 | tf_op jit(solution)/shard_map/all_to_all | solution.py:64
  313.9 1.6 copy.25
  315.4 0.5 broadcast.91
  316.0 0.7 reduce.7
  316.7 0.1 eq.92
  316.8 0.7 reduce.6
  317.6 0.1 eq.96
  317.7 13.1 %copy.40 = f32[16,8,128,128]{3,1,2,0:T(8,128)} copy(f32[16,8,128,128]{3,2,1,0:T(8,128)} %bitcast.55) | data formatting | bytes 16777216
  330.9 9.0 %copy.24 = f32[16384,128]{1,0:T(8,128)} copy(f32[16384,128]{0,1:T(8,128)} %bitcast.57) | data formatting | bytes 16777216 | tf_op jit(solution)/shard_map/dot_general | solution.py:40
  339.9 12.1 %fusion.15 = f32[16,8,128,128]{3,1,2,0:T(8,128)} fusion(f32[128,128,128,1]{2,1,0,3:T(8,128)} %bitcast.56, f32[128,8]{0,1:T(8,128)S(1)} %fusion.25, f32[128,16]{0,1:T(8,128)S(1)} %fusion.24), kind=kOutput, calls=%fused_computation.15 | convolution fusion | flops 3221241856 | bytes 16789504 | tf_op jit(solution)/shard_map/dot_general | solution.py:40
  351.9 16.5 %all-to-all-done.3 = f32[64,256,32]{1,2,0:T(8,128)S(1)} async-done(((f32[64,256,32]{1,2,0:T(8,128)}), f32[64,256,32]{1,2,0:T(8,128)S(1)}, u32[]{:S(2)}, u32[]{:S(2)}) %all-to-all-start.3) | async-done | bytes 2097184 | tf_op jit(solution)/shard_map/all_to_all | solution.py:64
  368.4 17.8 %fusion.8 = f32[256,1024]{0,1:T(8,128)} fusion(f32[256,1024]{0,1:T(8,128)S(1)} %copy.25, f32[256,2048]{0,1:T(8,128)S(1)} %bitcast.58, f32[256,8,8,128]{3,2,1,0:T(8,128)} %bitcast.54), kind=kOutput, calls=%fused_computation.7 | convolution fusion | flops 6442713088 | bytes 12582912 | tf_op jit(solution)/shard_map/dot_general | solution.py:62
  386.2 2.5 copy.26
  (4 shorter events, 0.0 us)
Async XLA Ops:
  6.5 61.3 %all-gather.2.cloned.1.call-start = ((), (), s32[]{:S(2)}) async-start(), calls=%async_computation.4 | async-start | bytes 4718592 | tf_op jit(solution)/shard_map/all_gather | solution.py:51
  11.9 29.2 %all-to-all-start = ((s32[64,1,2]{2,1,0:T(1,128)}), s32[64,1,2]{2,1,0:T(1,128)S(1)}, u32[]{:S(2)}, u32[]{:S(2)}) async-start(s32[64,1,2]{2,1,0:T(1,128)} %copy.20), calls=%async_computation | async-start | bytes 65536 | tf_op jit(solution)/shard_map/all_to_all | solution.py:55
  41.1 43.6 %all-to-all-start.1 = ((s32[64,1,2]{2,1,0:T(1,128)}), s32[64,1,2]{2,1,0:T(1,128)S(1)}, u32[]{:S(2)}, u32[]{:S(2)}) async-start(s32[64,1,2]{2,1,0:T(1,128)} %copy.21), calls=%async_computation.1 | async-start | bytes 65536 | tf_op jit(solution)/shard_map/all_to_all | solution.py:56
  84.7 205.2 %copy-start = (f32[256,32]{0,1:T(8,128)S(1)}, f32[256,32]{0,1:T(8,128)}, u32[]{:S(2)}) copy-start(f32[256,32]{0,1:T(8,128)} %param.7) | copy-start | bytes 98308
  291.5 76.9 %all-to-all-start.3 = ((f32[64,256,32]{1,2,0:T(8,128)}), f32[64,256,32]{1,2,0:T(8,128)S(1)}, u32[]{:S(2)}, u32[]{:S(2)}) async-start(f32[64,256,32]{1,2,0:T(8,128)} %stack.2), calls=%async_computation.3 | async-start | bytes 4194304 | tf_op jit(solution)/shard_map/all_to_all | solution.py:64
Sparse Core Ops, SparseCore 0:
  9.4 58.3 all-gather.1
